TPU v7x, 128 devices: a whole 4x4x4 slice. The times are simulated.
128 devices in a mesh: ent: 8 (over y, core), grp: 16 (over x, z).
Axes of the slice: x: 4, y: 4, z: 4, core: 2. Of those that a mesh axis runs over, the one named last changes fastest.
Arguments:
- table: float32 [262144, 512], P(('ent', 'grp')), may hold values from -6 to 6
- touch_owner: int32 [65536, 1], P(('ent', 'grp')), may hold values from 0 to 127; in each aligned block of 512 rows (0 to 511, 512 to 1023, ...) at most 8 rows name the same one
- touch_local: int32 [65536], P(('ent', 'grp')), may hold values from 0 to 2047
- query_rel: int32 [32768], P(('ent', 'grp')), may hold values from 0 to 821
- neg_local: int32 [32768], P(('ent', 'grp')), may hold values from 0 to 2047
- rel_table: bfloat16 [822, 512], replicated, may hold values from -6 to 6
- in_gain: float32 [512], replicated, may hold values from 0.1 to 1.9
- out_gain: float32 [512], replicated, may hold values from 0.1 to 1.9
- w_gate: bfloat16 [512, 2048], replicated, may hold values from -0.25 to 0.25
- w_up: bfloat16 [512, 2048], replicated, may hold values from -0.25 to 0.25
- w_down: bfloat16 [2048, 512], replicated, may hold values from -0.125 to 0.125
Outputs:
- table_grad: float32 [262144, 512], P(('ent', 'grp'))
Inputs may be any that keep to these rules, and one draw needn't show every extreme that they name: `touch_owner`: in each device's block of 512 references no owner is named more than 8 times, a bound that some block reaches.
All inputs are finite; a program needn't handle non-finite values.
Results may differ from a plain program's by a relative error of at most 0.0085.
Values may be sent and summed in bfloat16 or wider, within the bound.
A program may use at most 128 MiB of HBM per device.

v0:
```python
import math

import jax
import jax.numpy as jnp
from jax import lax
from jax.sharding import PartitionSpec as P

POS_WEIGHT = 64


norm_eps = 1e-06


def encode(head_rows, rel_rows, in_gain, out_gain, w_gate, w_up, w_down):
    base_sum = head_rows + rel_rows
    normed = (
        base_sum
        * lax.rsqrt(jnp.mean(base_sum * base_sum, axis=-1, keepdims=True) + norm_eps)
        * in_gain
    ).astype(jnp.bfloat16)
    gate_proj = jnp.dot(normed, w_gate, preferred_element_type=jnp.float32)
    up_proj = jnp.dot(normed, w_up, preferred_element_type=jnp.float32)
    hidden = (jax.nn.silu(gate_proj) * up_proj).astype(jnp.bfloat16)
    mixed_sum = base_sum + jnp.dot(hidden, w_down, preferred_element_type=jnp.float32)
    return (
        mixed_sum
        * lax.rsqrt(jnp.mean(mixed_sum * mixed_sum, axis=-1, keepdims=True) + norm_eps)
        * out_gain
    )


def per_device(
    table,
    touch_owner,
    touch_local,
    query_rel,
    neg_local,
    rel_table,
    in_gain,
    out_gain,
    w_gate,
    w_up,
    w_down,
):
    ent_count = lax.axis_size("ent")
    grp_count = lax.axis_size("grp")
    dev_count = ent_count * grp_count
    ref_count = touch_local.shape[0]
    queries = ref_count // 2
    capacity = 2 * ref_count // dev_count
    feat_width = table.shape[1]
    inv_scale = 1.0 / math.sqrt(feat_width)
    owners = touch_owner[:, 0]
    owner_hits = (owners[:, None] == jnp.arange(dev_count, dtype=jnp.int32)[None, :]).astype(
        jnp.int32
    )
    placed = jnp.sum(jnp.cumsum(owner_hits, axis=0) * owner_hits, axis=1) - 1
    slot_index = owners * capacity + placed
    requests = (
        jnp.zeros((dev_count * capacity,), jnp.int32)
        .at[slot_index]
        .set(touch_local)
        .reshape(dev_count, capacity)
    )
    wanted = lax.all_to_all(requests, ("ent", "grp"), split_axis=0, concat_axis=0, tiled=True)
    looked = table[wanted.reshape(-1)].astype(jnp.bfloat16)
    fetched = lax.all_to_all(
        looked.reshape(wanted.shape + (feat_width,)),
        ("ent", "grp"),
        split_axis=0,
        concat_axis=0,
        tiled=True,
    )
    gathered = fetched.reshape(dev_count * capacity, feat_width)[slot_index]
    head_rows = gathered[:queries]
    ctx_rows = gathered[queries:]
    rel_onehot = (
        query_rel[:, None] == jnp.arange(rel_table.shape[0], dtype=jnp.int32)[None, :]
    ).astype(jnp.bfloat16)
    rel_rows = jnp.dot(rel_onehot, rel_table, preferred_element_type=jnp.float32)

    def forward(head_f):
        return encode(head_f, rel_rows, in_gain, out_gain, w_gate, w_up, w_down)

    query_vec, pullback = jax.vjp(forward, head_rows.astype(jnp.float32))
    query_bf = query_vec.astype(jnp.bfloat16)
    neg_rows = table[neg_local].astype(jnp.bfloat16)
    negatives = lax.all_gather(neg_rows, "grp", axis=0, tiled=True)
    scores = jnp.dot(query_bf, negatives.T, preferred_element_type=jnp.float32) * inv_scale
    neg_weight = (jax.nn.sigmoid(scores) * inv_scale).astype(jnp.bfloat16)
    neg_query_grad = jnp.dot(neg_weight, negatives, preferred_element_type=jnp.float32)
    neg_grad = lax.psum_scatter(
        jnp.dot(neg_weight.T, query_bf, preferred_element_type=jnp.float32).astype(jnp.bfloat16),
        "grp",
        scatter_dimension=0,
        tiled=True,
    ).astype(jnp.float32)
    ctx_f = ctx_rows.astype(jnp.float32)
    pos_score = jnp.sum(query_vec * ctx_f, axis=-1) * inv_scale
    pos_weight = POS_WEIGHT * (jax.nn.sigmoid(pos_score) - 1.0) * inv_scale
    query_grad = neg_query_grad + pos_weight[:, None] * ctx_f
    ctx_grad = pos_weight[:, None] * query_vec
    head_grad = pullback(query_grad)[0]
    ref_grads = jnp.concatenate([head_grad, ctx_grad], axis=0)
    outgoing = (
        jnp.zeros((dev_count * capacity, feat_width), jnp.float32).at[slot_index].set(ref_grads)
    )
    returned = lax.all_to_all(
        outgoing.reshape(dev_count, capacity, feat_width),
        ("ent", "grp"),
        split_axis=0,
        concat_axis=0,
        tiled=True,
    )
    table_grad = jnp.zeros(table.shape, jnp.float32)
    table_grad = table_grad.at[wanted.reshape(-1)].add(returned.reshape(-1, feat_width))
    table_grad = table_grad.at[neg_local].add(neg_grad)
    return table_grad


def solution(mesh):
    return jax.shard_map(
        per_device,
        mesh=mesh,
        in_specs=(
            P(("ent", "grp"), None),
            P(("ent", "grp"), None),
            P(("ent", "grp")),
            P(("ent", "grp")),
            P(("ent", "grp")),
            P(),
            P(),
            P(),
            P(),
            P(),
            P(),
        ),
        out_specs=P(("ent", "grp"), None),
        check_vma=False,
    )
```

profile of v0, /device:TPU:1, one launch (start us, length us, event | category | flops | bytes accessed | tf_op | source)
XLA Modules:
  0.0 202.2 jit_solution(5347071745434437954)
XLA Ops:
  6.5 0.0 copy-start
  6.5 0.8 compare_select_fusion.2
  7.4 4.1 %gather_fusion.2 = bf16[256,512]{1,0:T(8,128)(2,1)} fusion(f32[2048,512]{1,0:T(8,128)} %param.11, s32[1024]{0:T(1024)S(1)} %pad_clamp_fusion), kind=kCustom, calls=%fused_computation.2 | custom fusion | bytes 525312 | tf_op jit(solution)/shard_map/gather | solution.py:87
  11.5 0.0 all-gather.2.cloned.1.call-update
  11.5 0.1 copy.15
  11.7 0.2 fusion.40
  12.0 0.2 fusion.39
  12.2 2.6 %scatter_custom_fusion = s32[1024]{0:T(1024)S(1)} fusion(s32[512]{0:T(512)S(1)} %bitcast.49, s32[512]{0:T(512)} %param.13, s32[]{:T(128)} %constant.14.clone.1), kind=kCustom, calls=%fused_computation.79 | custom fusion | bytes 4608 | tf_op jit(solution)/shard_map/scatter | solution.py:62
  14.8 0.1 all_to_all.12
  14.9 20.9 %all_to_all.19 = s32[128,1,8]{2,1,0:T(1,128)S(1)} all-to-all(s32[128,1,8]{2,1,0:T(1,128)S(1)} %bitcast.43), channel_id=1, replica_groups=mesh['ent'=8,'grp'=16] {'ent','grp'}, dimensions={0} | all-to-all | bytes 8192 | tf_op jit(solution)/shard_map/all_to_all | solution.py:65
  35.8 0.5 broadcast.224
  36.3 0.8 reduce.3
  37.1 0.1 reshape.119
  37.2 7.3 %gather_fusion = bf16[1024,512]{1,0:T(8,128)(2,1)} fusion(f32[2048,512]{1,0:T(8,128)} %param.11, s32[1024]{0:T(1024)S(1)} %broadcast_clamp_fusion), kind=kCustom, calls=%fused_computation | custom fusion | bytes 2101248 | tf_op jit(solution)/shard_map/gather | solution.py:66
  44.5 4.6 %all-to-all-start.1 = ((bf16[128,8,512]{2,1,0:T(8,128)(2,1)}), bf16[128,8,512]{2,1,0:T(8,128)(2,1)S(1)}, u32[]{:S(2)}, u32[]{:S(2)}) async-start(bf16[128,8,512]{2,1,0:T(8,128)(2,1)} %bitcast.40), calls=%async_computation.1 | async-start | bytes 2097152 | tf_op jit(solution)/shard_map/all_to_all | solution.py:67
  49.1 0.2 reduce-scatter.2.cloned.1.call-start
  49.4 29.8 %all-to-all-done.1 = bf16[128,8,512]{2,1,0:T(8,128)(2,1)S(1)} async-done(((bf16[128,8,512]{2,1,0:T(8,128)(2,1)}), bf16[128,8,512]{2,1,0:T(8,128)(2,1)S(1)}, u32[]{:S(2)}, u32[]{:S(2)}) %all-to-all-start.1) | async-done | bytes 1048608 | tf_op jit(solution)/shard_map/all_to_all | solution.py:67
  79.2 2.6 %gather_fusion.1 = bf16[512,512]{1,0:T(8,128)(2,1)} fusion(bf16[1024,512]{1,0:T(8,128)(2,1)S(1)} %bitcast.38, s32[1024]{0:T(1024)S(1)} %pad_clamp_fusion.1), kind=kCustom, calls=%fused_computation.1 | custom fusion | bytes 1050624 | tf_op jit(solution)/shard_map/gather | solution.py:74
  81.8 1.8 multiply_reduce_fusion.3
  83.6 0.0 copy-start.3
  83.7 2.5 %fusion.53 = f32[256,2048]{1,0:T(8,128)S(1)} fusion(bf16[512,2048]{1,0:T(8,128)(2,1)} %param.19, f32[256,512]{1,0:T(8,128)S(1)} %get-tuple-element.8, f32[512]{0:T(512)S(1)} %copy-done.9, f32[256]{0:T(256)S(1)} %fusion.45), kind=kOutput, calls=%fused_computation.93 | convolution fusion | flops 537264128 | bytes 4721664 | tf_op jit(solution)/shard_map/jvp()/dot_general | solution.py:21
  86.1 0.0 copy-done.3
  86.2 0.0 copy-start.5
  86.2 0.8 fusion.52
  86.9 0.6 copy-done.5
  87.5 0.9 multiply_reduce_fusion.2
  88.4 0.5 copy-done.7
  88.9 0.0 copy-done.10
  88.9 3.8 %fusion.5 = bf16[256,4096]{1,0:T(8,128)(2,1)S(1)} fusion(bf16[4096,512]{1,0:T(8,128)(2,1)} %all-gather.2.cloned.1.call-done, f32[256,512]{1,0:T(8,128)S(1)} %get-tuple-element.10, f32[512]{0:T(512)S(1)} %copy-done.10, f32[256]{0:T(256)S(1)} %fusion.46), kind=kOutput, calls=%fused_computation.14 | convolution fusion | flops 1080426496 | bytes 6818816 | tf_op jit(solution)/shard_map/dot_general | solution.py:89
  92.7 1.3 copy-done.1
  94.0 3.3 %convolution_convert_fusion = bf16[4096,512]{1,0:T(8,128)(2,1)} fusion(bf16[256,4096]{1,0:T(8,128)(2,1)S(1)} %fusion.5, f32[256,512]{1,0:T(8,128)S(1)} %get-tuple-element.10, f32[512]{0:T(512)S(1)} %copy-done.10, f32[256]{0:T(256)S(1)} %fusion.46), kind=kOutput, calls=%fused_computation.7 | convolution fusion | flops 1076232192 | bytes 6818816 | tf_op jit(solution)/shard_map/dot_general | solution.py:93
  97.2 0.0 reduce-scatter.2.cloned.1.call-update
  97.3 1.2 fusion.31
  98.5 4.3 %multiply_reduce_fusion.1 = (f32[256]{0:T(256)S(1)}, f32[256,512]{1,0:T(8,128)S(1)}) fusion(f32[256,512]{1,0:T(8,128)S(1)} %get-tuple-element.10, f32[512]{0:T(512)S(1)} %copy-done.10, bf16[512,512]{1,0:T(8,128)(2,1)} %gather_fusion.1, f32[256]{0:T(256)S(1)} %add_multiply_fusion, bf16[256,4096]{1,0:T(8,128)(2,1)} %copy-done.1, ...), kind=kOutput, calls=%fused_computation.56 | convolution fusion | flops 1074528000 | bytes 7606272 | tf_op jit(solution)/shard_map/dot_general | solution.py:91
  102.8 0.0 copy-start.2
  102.8 0.0 copy-start.6
  102.9 0.8 convolution_convert_fusion.1
  103.7 0.8 copy-done.2
  104.5 0.6 copy-done.6
  105.1 1.1 fusion.18
  106.2 0.5 copy-done.4
  106.7 1.1 multiply_reduce_fusion
  107.8 1.3 add_add_fusion
  109.1 4.4 %scatter_custom_fusion.1 = f32[1024,512]{1,0:T(8,128)} fusion(s32[512]{0:T(512)S(1)} %bitcast.51, f32[256,512]{1,0:T(8,128)} %get-tuple-element.6, f32[]{:T(128)} %constant.48, f32[256,512]{1,0:T(8,128)} %get-tuple-element.5, f32[]{:T(128)} %constant.13.clone.1), kind=kCustom, calls=%fused_computation.40 | custom fusion | flops 262144 | bytes 3145736 | tf_op jit(solution)/shard_map/scatter | solution.py:106
  113.5 38.8 %all_to_all.20 = f32[128,8,512]{2,1,0:T(8,128)} all-to-all(f32[128,8,512]{2,1,0:T(8,128)} %bitcast.39), channel_id=1, replica_groups=mesh['ent'=8,'grp'=16] {'ent','grp'}, dimensions={0} | all-to-all | bytes 4194304 | tf_op jit(solution)/shard_map/all_to_all | solution.py:108
  152.3 9.6 %scatter_custom_fusion.2 = f32[2048,512]{1,0:T(8,128)} fusion(s32[1024]{0:T(1024)S(1)} %bitcast.48, f32[128,8,512]{2,1,0:T(8,128)} %all_to_all.20, f32[]{:T(128)} %constant.13.clone.1), kind=kCustom, calls=%fused_computation.23 | custom fusion | flops 524288 | bytes 6291460 | tf_op jit(solution)/shard_map/scatter-add | solution.py:116
  161.9 26.8 %reduce-scatter.2.cloned.1.call-done = bf16[256,512]{1,0:T(8,128)(2,1)} async-done(((bf16[4096,512]{1,0:T(8,128)(2,1)}), bf16[256,512]{1,0:T(8,128)(2,1)}) %reduce-scatter.2.cloned.1.call-update) | async-done | bytes 262160 | tf_op jit(solution)/shard_map/reduce_scatter | solution.py:92
  188.7 6.7 %scatter_custom_fusion.3 = f32[2048,512]{1,0:T(8,128)} fusion(f32[2048,512]{1,0:T(8,128)} %scatter_custom_fusion.2, s32[256]{0:T(256)S(1)} %compare_select_fusion.2, bf16[256,512]{1,0:T(8,128)(2,1)} %reduce-scatter.2.cloned.1.call-done), kind=kCustom, calls=%fused_computation.53 | custom fusion | flops 262144 | bytes 4456448 | tf_op jit(solution)/shard_map/scatter-add | solution.py:117
  (32 shorter events, 0.2 us)
Async XLA Ops:
  6.5 80.9 %copy-start = (bf16[2048,512]{1,0:T(8,128)(2,1)S(1)}, bf16[2048,512]{1,0:T(8,128)(2,1)}, u32[]{:S(2)}) copy-start(bf16[2048,512]{1,0:T(8,128)(2,1)} %param.21) | copy-start | bytes 6291460
  6.5 5.0 %copy-start.11 = (s32[512,1]{0,1:T(1,128)S(1)}, s32[512,1]{0,1:T(1,128)}, u32[]{:S(2)}) copy-start(s32[512,1]{0,1:T(1,128)} %param.12) | copy-start | bytes 6148
  6.5 82.3 %all-gather.2.cloned.1.call-start = ((), (), s32[]{:S(2)}) async-start(), calls=%async_computation.4 | async-start | bytes 4456448 | tf_op jit(solution)/shard_map/all_gather | solution.py:88
  44.5 34.7 %all-to-all-start.1 = ((bf16[128,8,512]{2,1,0:T(8,128)(2,1)}), bf16[128,8,512]{2,1,0:T(8,128)(2,1)S(1)}, u32[]{:S(2)}, u32[]{:S(2)}) async-start(bf16[128,8,512]{2,1,0:T(8,128)(2,1)} %bitcast.40), calls=%async_computation.1 | async-start | bytes 2097152 | tf_op jit(solution)/shard_map/all_to_all | solution.py:67
  49.1 139.6 %reduce-scatter.2.cloned.1.call-start = ((), (), s32[]{:S(2)}) async-start(), calls=%async_computation.5 | async-start | bytes 4456448 | tf_op jit(solution)/shard_map/reduce_scatter | solution.py:92
  79.2 2.6 %copy-start.12 = (s32[256]{0:T(256)S(1)}, s32[256]{0:T(256)}, u32[]{:S(2)}) copy-start(s32[256]{0:T(256)} %param.14) | copy-start | bytes 3076
  79.2 4.4 %copy-start.9 = (f32[512]{0:T(512)S(1)}, f32[512]{0:T(512)}, u32[]{:S(2)}) copy-start(f32[512]{0:T(512)} %param.17) | copy-start | bytes 6148
  83.6 2.5 %copy-start.3 = (bf16[512,2048]{1,0:T(8,128)(2,1)S(1)}, bf16[512,2048]{1,0:T(8,128)(2,1)}, u32[]{:S(2)}) copy-start(bf16[512,2048]{1,0:T(8,128)(2,1)} %param.20) | copy-start | bytes 6291460
  86.2 1.3 copy-start.5
  87.5 1.4 copy-start.7
  87.5 1.4 copy-start.10
  92.7 1.3 copy-start.1
  98.5 5.2 %copy-start.8 = (f32[256,2048]{1,0:T(8,128)S(1)}, f32[256,2048]{1,0:T(8,128)}, u32[]{:S(2)}) copy-start(f32[256,2048]{1,0:T(8,128)} %copy-done.7) | copy-start | bytes 6291460
  102.8 1.6 copy-start.2
  102.8 2.3 %copy-start.6 = (f32[256,2048]{1,0:T(8,128)S(1)}, f32[256,2048]{1,0:T(8,128)}, u32[]{:S(2)}) copy-start(f32[256,2048]{1,0:T(8,128)} %copy-done.5) | copy-start | bytes 6291460
  105.1 1.6 copy-start.4
Sparse Core Ops, SparseCore 0:
  11.7 65.8 all-gather.1
  97.4 91.2 reduce-scatter.1
where the time goes:
time: 204 us; the launch traced here: 202 us
  blocking collectives  59.7 us (29%)
  waiting for transfers between devices  56.7 us (28%)
  other arithmetic  25.4 us (12%)
  local copies, waits for them, and re-layouts  21.8 us (11%)
  matrix products  20.3 us (10%)
  between operations  13.6 us (7%)
  starting transfers between devices  4.8 us (2%)
    all_to_all x1, blocking collectives, per_device(): lax.all_to_all(outgoing.reshape(dev_count, capacity, feat_width), ('ent',...  38.8 us
    all_to_all x1, waiting for transfers between devices, per_device(): lax.all_to_all(looked.reshape(wanted.shape + (feat_width,)), ('ent', 'grp...  29.8 us
    reduce_scatter x1, waiting for transfers between devices, per_device(): lax.psum_scatter(jnp.dot(neg_weight.T, query_bf, preferred_element_type=j...  26.8 us
    all_to_all x1, blocking collectives, per_device(): lax.all_to_all(requests, ('ent', 'grp'), split_axis=0, concat_axis=0, til...  20.9 us
    scatter-add x1, other arithmetic, per_device(): table_grad.at[wanted.reshape(-1)].add(returned.reshape(-1, feat_width))  9.64 us
    gather x1, local copies, waits for them, and re-layouts, per_device(): looked = table[wanted.reshape(-1)].astype(jnp.bfloat16)  7.3 us
    scatter-add x1, other arithmetic, per_device(): table_grad = table_grad.at[neg_local].add(neg_grad)  6.67 us
    all_to_all x1, starting transfers between devices, per_device(): lax.all_to_all(looked.reshape(wanted.shape + (feat_width,)), ('ent', 'grp...  4.57 us
  transfers between devices with their start and end apart: 3, of which 2 were waited for; matrix products, arithmetic and copies ran while one was open for 22% of the time, Pallas kernels for 0%

commit v1 on v0

v1 whole, which is shorter than its diff:
```python
import functools
import math

import jax
import jax.numpy as jnp
from jax import lax
from jax.experimental import pallas as pl
from jax.experimental.pallas import tpu as pltpu
from jax.sharding import PartitionSpec as P

MESH = pl.DeviceIdType.MESH
POS_WEIGHT = 64
EPS = 1e-06
BF = jnp.bfloat16
F32 = jnp.float32
I32 = jnp.int32
ENT = 8
GRP = 16
SIDE = 4
DEV = ENT * GRP
CAP = 8
SLOTS = DEV * CAP
REFS = 512
Q = 256
D = 512
FF = 2048
FC = 512
NFC = FF // FC
ROWS = 2048
NREL = 822
INV = 1.0 / math.sqrt(D)


def nn(a, b):
    return lax.dot_general(a, b, (((1,), (0,)), ((), ())), preferred_element_type=F32)


def nt(a, b):
    return lax.dot_general(a, b, (((1,), (1,)), ((), ())), preferred_element_type=F32)


def iota(shape, axis):
    return lax.broadcasted_iota(I32, shape, axis)


def hot(mask):
    return jnp.where(mask, 1.0, 0.0).astype(BF)


def column(row):
    return jnp.transpose(jnp.broadcast_to(row, (128, row.shape[1])))


class Gather:
    def __init__(self, ref, send, recv, me_e, me_g):
        self.ref, self.send, self.recv, self.me_e = ref, send, recv, me_e
        self.x, self.z = me_g // SIDE, me_g % SIDE
        self.copies = []

    def block(self, h, a1, a2):
        dx, dz = (a1, a2) if h == 0 else (a2, a1)
        return ((self.x + (dx + SIDE)) % SIDE) * SIDE + (self.z + (dz + SIDE)) % SIDE

    def slot(self, h, a1, a2, q):
        return (h * 16 + (a1 % SIDE) * SIDE + a2 % SIDE) * 2 + q

    def rows(self, h, a1, a2, part):
        lo, n = {None: (0, 128), 0: (0, 64), 1: (64, 64)}[part]
        return self.ref.at[self.block(h, a1, a2), pl.ds(h * 128 + lo, n), :]

    def push(self, h, a1, a2, part, t1, t2):
        r1, r2 = (a1 - t1) % SIDE, (a2 - t2) % SIDE
        i = len(self.copies)
        src = self.rows(h, a1, a2, part)
        copy = pltpu.make_async_remote_copy(
            src_ref=src,
            dst_ref=src,
            send_sem=self.send.at[i],
            recv_sem=self.recv.at[self.slot(h, r1, r2, part or 0)],
            device_id=(self.me_e, self.block(h, t1, t2)),
            device_id_type=MESH,
        )
        copy.start()
        self.copies.append(copy)

    def wait(self, h, a1, a2, part):
        view = self.rows(h, a1, a2, part)
        pltpu.make_async_copy(view, view, self.recv.at[self.slot(h, a1, a2, part or 0)]).wait()

    def second(self, h, a1):
        self.push(h, a1, 0, None, 0, 1)
        self.push(h, a1, 0, None, 0, -1)

    def stage0(self):
        for h in (0, 1):
            self.push(h, 0, 0, None, 1, 0)
            self.push(h, 0, 0, None, -1, 0)
        for h in (0, 1):
            self.second(h, 0)

    def stage1(self):
        for h in (0, 1):
            self.wait(h, -1, 0, None)
            self.push(h, -1, 0, 0, 1, 0)
            self.wait(h, 1, 0, None)
            self.push(h, 1, 0, 1, -1, 0)
        for h in (0, 1):
            self.second(h, -1)
            self.second(h, 1)
        self.across(0)

    def across(self, a1):
        for h in (0, 1):
            self.wait(h, a1, -1, None)
            self.push(h, a1, -1, 0, 0, 1)
            self.wait(h, a1, 1, None)
            self.push(h, a1, 1, 1, 0, -1)

    def stage2(self):
        for h in (0, 1):
            self.wait(h, 2, 0, 0)
            self.wait(h, 2, 0, 1)
            self.second(h, 2)

    def stage3(self):
        self.across(-1)
        self.across(1)
        self.across(2)

    def finish(self):
        for h in (0, 1):
            for a1 in (0, -1, 1, 2):
                self.wait(h, a1, 2, 0)
                self.wait(h, a1, 2, 1)

    def drain(self):
        for copy in self.copies:
            copy.wait_send()


def step_kernel(
    owner_ref, local_ref, rel_ref, neg_ref, gin_ref, gout_ref, tab_hbm, relt_hbm, wg_hbm, wu_hbm, wd_hbm,
    idrow_out, grads_out, negg_out,
    tab_f, tab_b, relt, wg, wu, wd,
    ids_s, ids_r, col_s, rows_s, rows_r, outg, back,
    negs, qall, base_s, gate_s, up_s, qvec_s, mix_s, acc_s, ctx_s,
    load_sem, a2a_send, a2a_recv, nsend, nrecv, qsend, qrecv,
):
    me_e, me_g = lax.axis_index("ent"), lax.axis_index("grp")
    me = me_e * GRP + me_g

    barrier = pltpu.get_barrier_semaphore()

    def greet(j, carry):
        t = (me + j) % DEV
        pl.semaphore_signal(barrier, inc=1, device_id=(t // GRP, t % GRP), device_id_type=MESH)
        return carry

    lax.fori_loop(1, DEV, greet, 0)

    loads = [
        pltpu.make_async_copy(src, dst, load_sem.at[i])
        for i, (src, dst) in enumerate(
            ((tab_hbm, tab_f), (relt_hbm, relt), (wg_hbm, wg), (wu_hbm, wu), (wd_hbm, wd))
        )
    ]
    for load in loads:
        load.start()

    def exchange(n, src, dst):
        def send(j, carry):
            t = (me + j) % DEV
            pltpu.make_async_remote_copy(
                src_ref=src.at[t],
                dst_ref=dst.at[me],
                send_sem=a2a_send.at[n],
                recv_sem=a2a_recv.at[n],
                device_id=(t // GRP, t % GRP),
                device_id_type=MESH,
            ).start()
            return carry

        lax.fori_loop(1, DEV, send, 0)
        dst[me] = src[me]

    def wait_all(buf, sem):
        view = buf.at[pl.ds(0, DEV - 1)]
        pltpu.make_async_copy(view, view, sem).wait()

    owner = owner_ref[...]
    local = local_ref[...]
    owner_t = hot(iota((DEV, REFS), 0) == owner)
    before = nn(owner_t, hot(iota((REFS, REFS), 0) < iota((REFS, REFS), 1)))
    placed = jnp.sum(before * owner_t.astype(F32), axis=0, keepdims=True).astype(I32)
    slot_row = owner * CAP + placed
    at = iota((128, REFS), 0) == placed
    high = (local // 256).astype(F32)
    low = (local % 256).astype(F32)
    zero = jnp.zeros((128, REFS), F32)
    ids = (
        256.0 * nt(owner_t, jnp.where(at, high, zero).astype(BF))
        + nt(owner_t, jnp.where(at, low, zero).astype(BF))
        + nt(owner_t, hot(at))
        - 1.0
    )
    ids_s[...] = ids.reshape(DEV, 1, 128)

    pl.semaphore_wait(barrier, DEV - 1)
    exchange(0, ids_s, ids_r)

    loads[0].wait()

    def narrow(i, carry):
        part = pl.ds(pl.multiple_of(i * 256, 256), 256)
        tab_b[part, :] = tab_f[part, :].astype(BF)
        return carry

    lax.fori_loop(0, ROWS // 256, narrow, 0)
    neg_col = column(neg_ref[...].astype(F32))[:, :1].astype(I32)
    negs[me_g] = nn(hot(neg_col == iota((Q, ROWS), 1)), tab_b[...]).astype(BF)
    ag_n = Gather(negs, nsend, nrecv, me_e, me_g)
    ag_n.stage0()

    wait_all(ids_r, a2a_recv.at[0])
    asked = ids_r[...].reshape(DEV, 128)
    asked_high = jnp.floor(asked * (1.0 / 256.0))
    asked_low = asked - 256.0 * asked_high
    spread = hot((iota((SLOTS, DEV), 0) // CAP) == iota((SLOTS, DEV), 1))
    mine = (iota((SLOTS, 128), 0) % CAP) == iota((SLOTS, 128), 1)
    slot_high = jnp.where(mine, nn(spread, asked_high.astype(BF)), 0.0)
    slot_low = jnp.where(mine, nn(spread, asked_low.astype(BF)), 0.0)
    ids_col = jnp.sum(256.0 * slot_high + slot_low, axis=1, keepdims=True)
    col_s[...] = jnp.broadcast_to(ids_col, (SLOTS, 128))
    ones = jnp.ones((8, 128), BF)
    idrow_out[...] = 256.0 * nt(ones, slot_high.astype(BF)) + nt(ones, slot_low.astype(BF))

    def look(i, carry):
        part = pl.ds(pl.multiple_of(i * 256, 256), 256)
        want = col_s[part, :][:, :1].astype(I32)
        found = nn(hot(want == iota((256, ROWS), 1)), tab_b[...])
        rows_s[pl.ds(i * 32, 32)] = found.reshape(32, CAP, D).astype(BF)
        return carry

    lax.fori_loop(0, SLOTS // 256, look, 0)
    exchange(1, rows_s, rows_r)
    ag_n.stage1()

    loads[1].wait()
    rel_col = column(rel_ref[...].astype(F32))[:, :1].astype(I32)
    rel_rows = nn(hot(rel_col == iota((Q, NREL), 1)), relt[...])
    slot_col = column(slot_row.astype(F32))[:, :1].astype(I32)
    pick = hot(slot_col == iota((REFS, SLOTS), 1))

    wait_all(rows_r, a2a_recv.at[1])
    came = rows_r[...].astype(F32).reshape(SLOTS, D).astype(BF)
    fetched = nn(pick, came)
    ctx_s[...] = fetched[Q:]
    base = fetched[:Q] + rel_rows
    base_s[...] = base
    r1 = lax.rsqrt(jnp.mean(base * base, axis=-1, keepdims=True) + EPS)
    normed = (base * r1 * gin_ref[...]).astype(BF)
    acc_s[...] = jnp.zeros((Q, D), F32)
    for load in loads[2:]:
        load.wait()

    def ahead(i, carry):
        part = pl.ds(pl.multiple_of(i * FC, FC), FC)
        g = nn(normed, wg[:, part])
        u = nn(normed, wu[:, part])
        gate_s[:, part] = g
        up_s[:, part] = u
        hidden = (g * jax.nn.sigmoid(g) * u).astype(BF)
        acc_s[...] += nn(hidden, wd[part, :])
        return carry

    lax.fori_loop(0, NFC, ahead, 0)
    mixed = base_s[...] + acc_s[...]
    r2 = lax.rsqrt(jnp.mean(mixed * mixed, axis=-1, keepdims=True) + EPS)
    query_vec = mixed * r2 * gout_ref[...]
    mix_s[...] = mixed
    qvec_s[...] = query_vec
    qall[me_g] = query_vec.astype(BF)
    ag_q = Gather(qall, qsend, qrecv, me_e, me_g)
    ag_q.stage0()
    ag_n.stage2()
    ag_n.stage3()
    ag_n.finish()

    def against(own, everyone):
        def body(i, carry):
            block = everyone[i]
            scores = nt(own, block) * (0.5 * INV)
            weight = ((0.5 * INV) * jnp.tanh(scores) + (0.5 * INV)).astype(BF)
            acc_s[...] += nn(weight, block)
            return carry

        acc_s[...] = jnp.zeros((Q, D), F32)
        lax.fori_loop(0, GRP, body, 0)

    against(qall[me_g], negs)
    ag_q.stage1()

    query_vec = qvec_s[...]
    ctx = ctx_s[...]
    pos_score = jnp.sum(query_vec * ctx, axis=-1, keepdims=True) * INV
    pos_weight = POS_WEIGHT * (jax.nn.sigmoid(pos_score) - 1.0) * INV
    query_grad = acc_s[...] + pos_weight * ctx
    ctx_grad = pos_weight * query_vec
    mixed = mix_s[...]
    r2 = lax.rsqrt(jnp.mean(mixed * mixed, axis=-1, keepdims=True) + EPS)
    t2 = query_grad * gout_ref[...]
    d_mixed = r2 * (t2 - mixed * (r2 * r2 * jnp.mean(t2 * mixed, axis=-1, keepdims=True)))
    d_mixed_b = d_mixed.astype(BF)
    acc_s[...] = jnp.zeros((Q, D), F32)

    def behind(i, carry):
        part = pl.ds(pl.multiple_of(i * FC, FC), FC)
        g = gate_s[:, part]
        u = up_s[:, part]
        s = jax.nn.sigmoid(g)
        dh = nt(d_mixed_b, wd[part, :]).astype(BF).astype(F32)
        du = (dh * (g * s)).astype(BF)
        dg = (dh * u * (s * (1.0 + g * (1.0 - s)))).astype(BF)
        acc_s[...] += nt(dg, wg[:, part]) + nt(du, wu[:, part])
        return carry

    lax.fori_loop(0, NFC, behind, 0)
    base = base_s[...]
    r1 = lax.rsqrt(jnp.mean(base * base, axis=-1, keepdims=True) + EPS)
    t1 = acc_s[...] * gin_ref[...]
    head_grad = d_mixed + r1 * (t1 - base * (r1 * r1 * jnp.mean(t1 * base, axis=-1, keepdims=True)))
    head_b = head_grad.astype(BF)
    ctx_b = ctx_grad.astype(BF)

    place = hot(iota((SLOTS, REFS), 0) == slot_row)
    out = nn(place[:, :Q], head_b) + nn(place[:, Q:], ctx_b)
    outg[...] = out.reshape(DEV, CAP, D).astype(BF)
    exchange(2, outg, back)
    ag_q.stage2()
    ag_q.stage3()
    ag_q.finish()

    against(negs[me_g], qall)
    total = acc_s[...]
    top = total.astype(BF)
    negg_out[:Q, :] = top
    negg_out[Q:, :] = (total - top.astype(F32)).astype(BF)

    wait_all(back, a2a_recv.at[2])
    grads_out[...] = back[...].astype(F32).reshape(SLOTS, D).astype(BF)
    wait_all(ids_s, a2a_send.at[0])
    wait_all(rows_s, a2a_send.at[1])
    wait_all(outg, a2a_send.at[2])
    ag_n.drain()
    ag_q.drain()


def place_kernel(idrow_ref, grads_ref, neg_ref, negg_ref, out_ref):
    first = pl.program_id(0) * 256
    slots = hot(iota((256, SLOTS), 0) + first == idrow_ref[...][:1, :].astype(I32))
    spans = hot(iota((256, Q), 0) + first == neg_ref[...])
    out_ref[...] = nn(slots, grads_ref[...]) + (nn(spans, negg_ref[:Q, :]) + nn(spans, negg_ref[Q:, :]))


def per_device(table, touch_owner, touch_local, query_rel, neg_local, rel_table, in_gain, out_gain, w_gate, w_up, w_down):
    neg_row = neg_local.reshape(1, Q)
    vmem = pl.BlockSpec(memory_space=pltpu.VMEM)
    hbm = pl.BlockSpec(memory_space=pl.ANY)
    idrow, grads, negg = pl.pallas_call(
        step_kernel,
        out_shape=(
            jax.ShapeDtypeStruct((8, SLOTS), F32),
            jax.ShapeDtypeStruct((SLOTS, D), BF),
            jax.ShapeDtypeStruct((2 * Q, D), BF),
        ),
        in_specs=[vmem] * 6 + [hbm] * 5,
        out_specs=(vmem, vmem, vmem),
        scratch_shapes=[
            pltpu.VMEM((ROWS, D), F32),
            pltpu.VMEM((ROWS, D), BF),
            pltpu.VMEM((NREL, D), BF),
            pltpu.VMEM((D, FF), BF),
            pltpu.VMEM((D, FF), BF),
            pltpu.VMEM((FF, D), BF),
            pltpu.VMEM((DEV, 1, 128), F32),
            pltpu.VMEM((DEV, 1, 128), F32),
            pltpu.VMEM((SLOTS, 128), F32),
            pltpu.VMEM((DEV, CAP, D), BF),
            pltpu.VMEM((DEV, CAP, D), BF),
            pltpu.VMEM((DEV, CAP, D), BF),
            pltpu.VMEM((DEV, CAP, D), BF),
            pltpu.VMEM((GRP, Q, D), BF),
            pltpu.VMEM((GRP, Q, D), BF),
            pltpu.VMEM((Q, D), F32),
            pltpu.VMEM((Q, FF), F32),
            pltpu.VMEM((Q, FF), F32),
            pltpu.VMEM((Q, D), F32),
            pltpu.VMEM((Q, D), F32),
            pltpu.VMEM((Q, D), F32),
            pltpu.VMEM((Q, D), F32),
            pltpu.SemaphoreType.DMA((5,)),
            pltpu.SemaphoreType.DMA((3,)),
            pltpu.SemaphoreType.DMA((3,)),
            pltpu.SemaphoreType.DMA((40,)),
            pltpu.SemaphoreType.DMA((64,)),
            pltpu.SemaphoreType.DMA((40,)),
            pltpu.SemaphoreType.DMA((64,)),
        ],
        compiler_params=pltpu.CompilerParams(
            collective_id=0, has_side_effects=True, vmem_limit_bytes=60 * 1024 * 1024
        ),
        name="step",
    )(
        touch_owner.reshape(1, REFS),
        touch_local.reshape(1, REFS),
        query_rel.reshape(1, Q),
        neg_row,
        in_gain.reshape(1, D),
        out_gain.reshape(1, D),
        table,
        rel_table,
        w_gate,
        w_up,
        w_down,
    )
    whole = lambda shape: pl.BlockSpec(shape, lambda i: (0, 0))
    return pl.pallas_call(
        place_kernel,
        grid=(ROWS // 256,),
        out_shape=jax.ShapeDtypeStruct((ROWS, D), F32),
        in_specs=[whole((8, SLOTS)), whole((SLOTS, D)), whole((1, Q)), whole((2 * Q, D))],
        out_specs=pl.BlockSpec((256, D), lambda i: (i, 0)),
        name="place",
    )(idrow, grads, neg_row, negg)


def solution(mesh):
    split = P(("ent", "grp"))
    rows = P(("ent", "grp"), None)
    return jax.shard_map(
        per_device,
        mesh=mesh,
        in_specs=(rows, rows, split, split, split, P(), P(), P(), P(), P(), P()),
        out_specs=rows,
        check_vma=False,
    )
```

time: 204 us -> 115 us (0.56)
  Pallas kernels: 0 us -> 114 us
  blocking collectives: 59.7 us -> 0 us
  waiting for transfers between devices: 56.7 us -> 0 us
  other arithmetic: 25.4 us -> 0 us
  local copies, waits for them, and re-layouts: 21.8 us -> 0 us
  matrix products: 20.3 us -> 0 us
  between operations: 13.6 us -> 0.01 us
  starting transfers between devices: 4.8 us -> 0 us
    pallas_call x0 -> x2, Pallas kernels: none -> 114 us  [the longest x1 107 us: per_device(): pl.pallas_call(step_kernel, out_shape=(jax.ShapeDtypeStruct((8, SLOTS), F...]
    all_to_all x2 -> x0, blocking collectives: 59.7 us -> none  [the longest x1 38.8 us: per_device(): lax.all_to_all(outgoing.reshape(dev_count, capacity, feat_width), ('ent',...]
    all_to_all x1 -> x0, waiting for transfers between devices: 29.8 us -> none  [per_device(): lax.all_to_all(looked.reshape(wanted.shape + (feat_width,)), ('ent', 'grp...]
    reduce_scatter x1 -> x0, waiting for transfers between devices: 26.8 us -> none  [per_device(): lax.psum_scatter(jnp.dot(neg_weight.T, query_bf, preferred_element_type=j...]
    dot_general x10 -> x0, matrix products: 20.3 us -> none  [the longest x1 4.34 us: per_device(): jnp.dot(neg_weight, negatives, preferred_element_type=jnp.float32)]
    scatter-add x2 -> x0, other arithmetic: 16.3 us -> none  [the longest x1 9.64 us: per_device(): table_grad.at[wanted.reshape(-1)].add(returned.reshape(-1, feat_width))]
    gather x3 -> x0, local copies, waits for them, and re-layouts: 14 us -> none  [the longest x1 7.3 us: per_device(): looked = table[wanted.reshape(-1)].astype(jnp.bfloat16)]
    all_to_all x1 -> x0, starting transfers between devices: 4.57 us -> none  [per_device(): lax.all_to_all(looked.reshape(wanted.shape + (feat_width,)), ('ent', 'grp...]
  transfers between devices with their start and end apart: 3 -> 0, of which waited for: 2 -> 0; matrix products, arithmetic and copies ran while one was open for 22% -> 0% of each run, Pallas kernels for 0% -> 0%
where the time goes in v1:
time: 115 us; the launch traced here: 114 us
  Pallas kernels  114 us (99%)
    pallas_call x1, Pallas kernels, per_device(): pl.pallas_call(step_kernel, out_shape=(jax.ShapeDtypeStruct((8, SLOTS), F...  107 us
    pallas_call x1, Pallas kernels, per_device(): pl.pallas_call(place_kernel, grid=(ROWS // 256,), out_shape=jax.ShapeDtyp...  7.46 us

profile of v1, /device:TPU:1, one launch (start us, length us, event | category | flops | bytes accessed | tf_op | source)
XLA Modules:
  0.0 114.4 jit_solution(8458609338190239770)
XLA Ops:
  0.0 106.9 %step.1 = (f32[8,1024]{1,0:T(8,128)}, bf16[1024,512]{1,0:T(8,128)(2,1)}, bf16[512,512]{1,0:T(8,128)(2,1)}) custom-call(s32[1,512]{1,0:T(1,128)} %bitcast.8, s32[1,512]{1,0:T(1,128)} %bitcast.9, s32[1,256]{1,0:T(1,128)} %bitcast.12, s32[1,256]{1,0:T(1,128)} %bitcast.6, f32[1,512]{1,0:T(1,128)} %bitcast.10, f32[1,512]{1,0:T(1,128)} %bitcast.11, ...), custom_call_target="tpu_custom_call" | custom-call | tf_op jit(solution)/shard_map/step/pallas_call | solution.py:369
  106.9 7.5 %place.1 = f32[2048,512]{1,0:T(8,128)} custom-call(f32[8,1024]{1,0:T(8,128)} %get-tuple-element.8.idrow_ref, bf16[1024,512]{1,0:T(8,128)(2,1)} %get-tuple-element.9.grads_ref, s32[1,256]{1,0:T(1,128)} %bitcast.7, bf16[512,512]{1,0:T(8,128)(2,1)} %get-tuple-element.10.negg_ref), custom_call_target="tpu_custom_call" | custom-call | tf_op jit(solution)/shard_map/place/pallas_call | solution.py:427

commit v2 on v1

--- a/solution.py
+++ b/solution.py
@@ -28,6 +28,7 @@
 NFC = FF // FC
 ROWS = 2048
 NREL = 822
+TILE = 512
 INV = 1.0 / math.sqrt(D)
 
 
@@ -107,7 +108,6 @@
         for h in (0, 1):
             self.second(h, -1)
             self.second(h, 1)
-        self.across(0)
 
     def across(self, a1):
         for h in (0, 1):
@@ -121,11 +121,6 @@
             self.wait(h, 2, 0, 0)
             self.wait(h, 2, 0, 1)
             self.second(h, 2)
-
-    def stage3(self):
-        self.across(-1)
-        self.across(1)
-        self.across(2)
 
     def finish(self):
         for h in (0, 1):
@@ -143,20 +138,33 @@
     idrow_out, grads_out, negg_out,
     tab_f, tab_b, relt, wg, wu, wd,
     ids_s, ids_r, col_s, rows_s, rows_r, outg, back,
-    negs, qall, base_s, gate_s, up_s, qvec_s, mix_s, acc_s, ctx_s,
-    load_sem, a2a_send, a2a_recv, nsend, nrecv, qsend, qrecv,
+    negs, qring, part_s, part_r, sums, base_s, gate_s, up_s, qvec_s, mix_s, acc_s, ctx_s,
+    load_sem, a2a_send, a2a_recv, nsend, nrecv, rsend, rrecv,
 ):
     me_e, me_g = lax.axis_index("ent"), lax.axis_index("grp")
     me = me_e * GRP + me_g
 
     barrier = pltpu.get_barrier_semaphore()
 
-    def greet(j, carry):
-        t = (me + j) % DEV
-        pl.semaphore_signal(barrier, inc=1, device_id=(t // GRP, t % GRP), device_id_type=MESH)
-        return carry
-
-    lax.fori_loop(1, DEV, greet, 0)
+    others = [lax.rem(me_g + k, GRP) for k in range(GRP)]
+
+    def each_peer(act, lo=0, hi=ENT):
+        def across(j, carry):
+            e = lax.rem(me_e + j, ENT)
+            for g in others[1:]:
+                act(e, g)
+            return carry
+
+        def along(j, carry):
+            act(lax.rem(me_e + j, ENT), me_g)
+            return carry
+
+        lax.fori_loop(lo, hi, across, 0)
+        lax.fori_loop(max(lo, 1), hi, along, 0)
+
+    each_peer(
+        lambda e, g: pl.semaphore_signal(barrier, inc=1, device_id=(e, g), device_id_type=MESH)
+    )
 
     loads = [
         pltpu.make_async_copy(src, dst, load_sem.at[i])
@@ -167,21 +175,20 @@
     for load in loads:
         load.start()
 
-    def exchange(n, src, dst):
-        def send(j, carry):
-            t = (me + j) % DEV
+    def exchange(n, src, dst, lo=0, hi=ENT):
+        def send(e, g):
             pltpu.make_async_remote_copy(
-                src_ref=src.at[t],
+                src_ref=src.at[e * GRP + g],
                 dst_ref=dst.at[me],
                 send_sem=a2a_send.at[n],
                 recv_sem=a2a_recv.at[n],
-                device_id=(t // GRP, t % GRP),
+                device_id=(e, g),
                 device_id_type=MESH,
             ).start()
-            return carry
-
-        lax.fori_loop(1, DEV, send, 0)
-        dst[me] = src[me]
+
+        each_peer(send, lo, hi)
+        if lo == 0:
+            dst[me] = src[me]
 
     def wait_all(buf, sem):
         view = buf.at[pl.ds(0, DEV - 1)]
@@ -205,9 +212,6 @@
     )
     ids_s[...] = ids.reshape(DEV, 1, 128)
 
-    pl.semaphore_wait(barrier, DEV - 1)
-    exchange(0, ids_s, ids_r)
-
     loads[0].wait()
 
     def narrow(i, carry):
@@ -219,6 +223,9 @@
     neg_col = column(neg_ref[...].astype(F32))[:, :1].astype(I32)
     negs[me_g] = nn(hot(neg_col == iota((Q, ROWS), 1)), tab_b[...]).astype(BF)
     ag_n = Gather(negs, nsend, nrecv, me_e, me_g)
+
+    pl.semaphore_wait(barrier, DEV - 1)
+    exchange(0, ids_s, ids_r)
     ag_n.stage0()
 
     wait_all(ids_r, a2a_recv.at[0])
@@ -234,6 +241,8 @@
     ones = jnp.ones((8, 128), BF)
     idrow_out[...] = 256.0 * nt(ones, slot_high.astype(BF)) + nt(ones, slot_low.astype(BF))
 
+    ag_n.stage1()
+
     def look(i, carry):
         part = pl.ds(pl.multiple_of(i * 256, 256), 256)
         want = col_s[part, :][:, :1].astype(I32)
@@ -243,7 +252,10 @@
 
     lax.fori_loop(0, SLOTS // 256, look, 0)
     exchange(1, rows_s, rows_r)
-    ag_n.stage1()
+    ag_n.across(0)
+    ag_n.stage2()
+    ag_n.across(-1)
+    ag_n.across(1)
 
     loads[1].wait()
     rel_col = column(rel_ref[...].astype(F32))[:, :1].astype(I32)
@@ -254,6 +266,7 @@
     wait_all(rows_r, a2a_recv.at[1])
     came = rows_r[...].astype(F32).reshape(SLOTS, D).astype(BF)
     fetched = nn(pick, came)
+    ag_n.across(2)
     ctx_s[...] = fetched[Q:]
     base = fetched[:Q] + rel_rows
     base_s[...] = base
@@ -279,26 +292,53 @@
     query_vec = mixed * r2 * gout_ref[...]
     mix_s[...] = mixed
     qvec_s[...] = query_vec
-    qall[me_g] = query_vec.astype(BF)
-    ag_q = Gather(qall, qsend, qrecv, me_e, me_g)
-    ag_q.stage0()
-    ag_n.stage2()
-    ag_n.stage3()
-    ag_n.finish()
-
-    def against(own, everyone):
-        def body(i, carry):
-            block = everyone[i]
+    x, z = ag_n.x, ag_n.z
+    query_b = query_vec.astype(BF)
+    ring = []
+
+    def hop(src, dst, sem, g):
+        copy = pltpu.make_async_remote_copy(
+            src_ref=src, dst_ref=dst, send_sem=rsend.at[sem], recv_sem=rrecv.at[sem],
+            device_id=(me_e, g), device_id_type=MESH,
+        )
+        copy.start()
+        ring.append(copy)
+
+    def arrive(view, sem):
+        pltpu.make_async_copy(view, view, rrecv.at[sem]).wait()
+
+    ahead_of = lambda i, k: lax.rem(i + k, SIDE)
+    rings = [
+        (z, ahead_of(z, 1), ahead_of(z, 3), x * SIDE + ahead_of(z, 1), x * SIDE + ahead_of(z, 3)),
+        (x, ahead_of(x, 1), ahead_of(x, 3), ahead_of(x, 1) * SIDE + z, ahead_of(x, 3) * SIDE + z),
+    ]
+    first, second = pl.ds(0, 128), pl.ds(128, 128)
+    for k, (own, _, _, after, before_me) in enumerate(rings):
+        qring[k, own] = query_b
+        hop(qring.at[k, own], qring.at[k, own], 8 * k, after)
+        hop(qring.at[k, own], qring.at[k, own], 8 * k + 1, before_me)
+
+    def against(own, blocks):
+        total = None
+        for block in blocks:
             scores = nt(own, block) * (0.5 * INV)
             weight = ((0.5 * INV) * jnp.tanh(scores) + (0.5 * INV)).astype(BF)
-            acc_s[...] += nn(weight, block)
-            return carry
-
-        acc_s[...] = jnp.zeros((Q, D), F32)
-        lax.fori_loop(0, GRP, body, 0)
-
-    against(qall[me_g], negs)
-    ag_q.stage1()
+            term = nn(weight, block)
+            total = term if total is None else total + term
+        return total
+
+    def neg_at(dx, dz):
+        return negs[lax.rem(x + (dx + SIDE), SIDE) * SIDE + lax.rem(z + (dz + SIDE), SIDE)]
+
+    def near(i, carry):
+        acc_s[...] += against(query_b, [neg_at(i - 1, dz) for dz in (-1, 0, 1)])
+        return carry
+
+    acc_s[...] = jnp.zeros((Q, D), F32)
+    lax.fori_loop(0, 3, near, 0)
+    ag_n.finish()
+    acc_s[...] += against(query_b, [neg_at(dx, 2) for dx in (-1, 0, 1)])
+    acc_s[...] += against(query_b, [neg_at(2, dz) for dz in (-1, 0, 1, 2)])
 
     query_vec = qvec_s[...]
     ctx = ctx_s[...]
@@ -324,7 +364,13 @@
         acc_s[...] += nt(dg, wg[:, part]) + nt(du, wu[:, part])
         return carry
 
-    lax.fori_loop(0, NFC, behind, 0)
+    lax.fori_loop(0, NFC // 2, behind, 0)
+    for k, (_, nxt, prev, after, before_me) in enumerate(rings):
+        arrive(qring.at[k, prev], 8 * k)
+        hop(qring.at[k, prev, first], qring.at[k, prev, first], 8 * k + 2, after)
+        arrive(qring.at[k, nxt], 8 * k + 1)
+        hop(qring.at[k, nxt, second], qring.at[k, nxt, second], 8 * k + 3, before_me)
+    lax.fori_loop(NFC // 2, NFC, behind, 0)
     base = base_s[...]
     r1 = lax.rsqrt(jnp.mean(base * base, axis=-1, keepdims=True) + EPS)
     t1 = acc_s[...] * gin_ref[...]
@@ -335,16 +381,37 @@
     place = hot(iota((SLOTS, REFS), 0) == slot_row)
     out = nn(place[:, :Q], head_b) + nn(place[:, Q:], ctx_b)
     outg[...] = out.reshape(DEV, CAP, D).astype(BF)
-    exchange(2, outg, back)
-    ag_q.stage2()
-    ag_q.stage3()
-    ag_q.finish()
-
-    against(negs[me_g], qall)
-    total = acc_s[...]
-    top = total.astype(BF)
-    negg_out[:Q, :] = top
-    negg_out[Q:, :] = (total - top.astype(F32)).astype(BF)
+    exchange(2, outg, back, 0, ENT // 2)
+
+    upper, lower = pl.ds(0, 64), pl.ds(64, 64)
+    for h in (0, 1):
+        arrive(qring.at[h, 0, first], 8 * h + 2)
+        arrive(qring.at[h, 0, second], 8 * h + 3)
+        own = jnp.concatenate(
+            [negs[ag_n.block(h, a, 0), h * 128 : h * 128 + 128] for a in (2, 1, -1, 0)], axis=0
+        )
+        terms = against(own, [qring[h, i] for i in range(SIDE)])
+        part_s[h, 0] = terms[:128].astype(BF)
+        sums[h] = terms[128:]
+        _, _, _, after, before_me = rings[1 - h]
+        hop(part_s.at[h, 0, upper], part_r.at[h, 0, upper], 8 * h + 4, after)
+        hop(part_s.at[h, 0, lower], part_r.at[h, 0, lower], 8 * h + 5, before_me)
+    exchange(2, outg, back, ENT // 2, ENT)
+    for h in (0, 1):
+        _, _, _, after, before_me = rings[1 - h]
+        arrive(part_r.at[h, 0, upper], 8 * h + 4)
+        part_s[h, 1, :64] = (sums[h, :64] + part_r[h, 0, :64].astype(F32)).astype(BF)
+        part_s[h, 1, 64:] = sums[h, 64:128].astype(BF)
+        hop(part_s.at[h, 1], part_r.at[h, 1], 8 * h + 6, after)
+        arrive(part_r.at[h, 0, lower], 8 * h + 5)
+        part_s[h, 2, :64] = sums[h, 128:192].astype(BF)
+        part_s[h, 2, 64:] = (sums[h, 192:256] + part_r[h, 0, 64:].astype(F32)).astype(BF)
+        hop(part_s.at[h, 2], part_r.at[h, 2], 8 * h + 7, before_me)
+    for h in (0, 1):
+        arrive(part_r.at[h, 1], 8 * h + 6)
+        arrive(part_r.at[h, 2], 8 * h + 7)
+        total = sums[h, 256:] + (part_r[h, 1].astype(F32) + part_r[h, 2].astype(F32))
+        negg_out[h * 128 : h * 128 + 128, :] = total.astype(BF)
 
     wait_all(back, a2a_recv.at[2])
     grads_out[...] = back[...].astype(F32).reshape(SLOTS, D).astype(BF)
@@ -352,14 +419,15 @@
     wait_all(rows_s, a2a_send.at[1])
     wait_all(outg, a2a_send.at[2])
     ag_n.drain()
-    ag_q.drain()
+    for copy in ring:
+        copy.wait_send()
 
 
 def place_kernel(idrow_ref, grads_ref, neg_ref, negg_ref, out_ref):
-    first = pl.program_id(0) * 256
-    slots = hot(iota((256, SLOTS), 0) + first == idrow_ref[...][:1, :].astype(I32))
-    spans = hot(iota((256, Q), 0) + first == neg_ref[...])
-    out_ref[...] = nn(slots, grads_ref[...]) + (nn(spans, negg_ref[:Q, :]) + nn(spans, negg_ref[Q:, :]))
+    start = pl.program_id(0) * TILE
+    slots = hot(iota((TILE, SLOTS), 0) + start == idrow_ref[...][:1, :].astype(I32))
+    spans = hot(iota((TILE, Q), 0) + start == neg_ref[...])
+    out_ref[...] = nn(slots, grads_ref[...]) + nn(spans, negg_ref[...])
 
 
 def per_device(table, touch_owner, touch_local, query_rel, neg_local, rel_table, in_gain, out_gain, w_gate, w_up, w_down):
@@ -371,7 +439,7 @@
         out_shape=(
             jax.ShapeDtypeStruct((8, SLOTS), F32),
             jax.ShapeDtypeStruct((SLOTS, D), BF),
-            jax.ShapeDtypeStruct((2 * Q, D), BF),
+            jax.ShapeDtypeStruct((Q, D), BF),
         ),
         in_specs=[vmem] * 6 + [hbm] * 5,
         out_specs=(vmem, vmem, vmem),
@@ -390,7 +458,10 @@
             pltpu.VMEM((DEV, CAP, D), BF),
             pltpu.VMEM((DEV, CAP, D), BF),
             pltpu.VMEM((GRP, Q, D), BF),
-            pltpu.VMEM((GRP, Q, D), BF),
+            pltpu.VMEM((2, SIDE, Q, D), BF),
+            pltpu.VMEM((2, 3, 128, D), BF),
+            pltpu.VMEM((2, 3, 128, D), BF),
+            pltpu.VMEM((2, 384, D), F32),
             pltpu.VMEM((Q, D), F32),
             pltpu.VMEM((Q, FF), F32),
             pltpu.VMEM((Q, FF), F32),
@@ -403,8 +474,8 @@
             pltpu.SemaphoreType.DMA((3,)),
             pltpu.SemaphoreType.DMA((40,)),
             pltpu.SemaphoreType.DMA((64,)),
-            pltpu.SemaphoreType.DMA((40,)),
-            pltpu.SemaphoreType.DMA((64,)),
+            pltpu.SemaphoreType.DMA((16,)),
+            pltpu.SemaphoreType.DMA((16,)),
         ],
         compiler_params=pltpu.CompilerParams(
             collective_id=0, has_side_effects=True, vmem_limit_bytes=60 * 1024 * 1024
@@ -426,10 +497,10 @@
     whole = lambda shape: pl.BlockSpec(shape, lambda i: (0, 0))
     return pl.pallas_call(
         place_kernel,
-        grid=(ROWS // 256,),
+        grid=(ROWS // TILE,),
         out_shape=jax.ShapeDtypeStruct((ROWS, D), F32),
-        in_specs=[whole((8, SLOTS)), whole((SLOTS, D)), whole((1, Q)), whole((2 * Q, D))],
-        out_specs=pl.BlockSpec((256, D), lambda i: (i, 0)),
+        in_specs=[whole((8, SLOTS)), whole((SLOTS, D)), whole((1, Q)), whole((Q, D))],
+        out_specs=pl.BlockSpec((TILE, D), lambda i: (i, 0)),
         name="place",
     )(idrow, grads, neg_row, negg)
 

time: 115 us -> 83.1 us (0.72)
  Pallas kernels: 114 us -> 83 us
    pallas_call x1, Pallas kernels: 107 us -> 77.2 us  [per_device(): pl.pallas_call(step_kernel, out_shape=(jax.ShapeDtypeStruct((8, SLOTS), F...]
    pallas_call x1, Pallas kernels: 7.46 us -> 5.81 us  [per_device(): pl.pallas_call(place_kernel, grid=(ROWS // TILE,), out_shape=jax.ShapeDty...]
where the time goes in v2:
time: 83.1 us; the launch traced here: 83 us
  Pallas kernels  83 us (100%)
    pallas_call x1, Pallas kernels, per_device(): pl.pallas_call(step_kernel, out_shape=(jax.ShapeDtypeStruct((8, SLOTS), F...  77.2 us
    pallas_call x1, Pallas kernels, per_device(): pl.pallas_call(place_kernel, grid=(ROWS // TILE,), out_shape=jax.ShapeDty...  5.81 us

profile of v2, /device:TPU:1, one launch (start us, length us, event | category | flops | bytes accessed | tf_op | source)
XLA Modules:
  0.0 83.0 jit_solution(13367025387860665547)
XLA Ops:
  0.0 77.2 %step.1 = (f32[8,1024]{1,0:T(8,128)}, bf16[1024,512]{1,0:T(8,128)(2,1)}, bf16[256,512]{1,0:T(8,128)(2,1)}) custom-call(s32[1,512]{1,0:T(1,128)} %bitcast.8, s32[1,512]{1,0:T(1,128)} %bitcast.9, s32[1,256]{1,0:T(1,128)} %bitcast.12, s32[1,256]{1,0:T(1,128)} %bitcast.6, f32[1,512]{1,0:T(1,128)} %bitcast.10, f32[1,512]{1,0:T(1,128)} %bitcast.11, ...), custom_call_target="tpu_custom_call" | custom-call | tf_op jit(solution)/shard_map/step/pallas_call | solution.py:437
  77.2 5.8 %place.1 = f32[2048,512]{1,0:T(8,128)} custom-call(f32[8,1024]{1,0:T(8,128)} %get-tuple-element.8.idrow_ref, bf16[1024,512]{1,0:T(8,128)(2,1)} %get-tuple-element.9.grads_ref, s32[1,256]{1,0:T(1,128)} %bitcast.7, bf16[256,512]{1,0:T(8,128)(2,1)} %get-tuple-element.10.negg_ref), custom_call_target="tpu_custom_call" | custom-call | tf_op jit(solution)/shard_map/place/pallas_call | solution.py:498

commit v3 on v2

--- a/solution.py
+++ b/solution.py
@@ -29,6 +29,7 @@
 ROWS = 2048
 NREL = 822
 TILE = 512
+LOOK = 512
 INV = 1.0 / math.sqrt(D)
 
 
@@ -107,7 +108,6 @@
             self.push(h, 1, 0, 1, -1, 0)
         for h in (0, 1):
             self.second(h, -1)
-            self.second(h, 1)
 
     def across(self, a1):
         for h in (0, 1):
@@ -134,46 +134,56 @@
 
 
 def step_kernel(
-    owner_ref, local_ref, rel_ref, neg_ref, gin_ref, gout_ref, tab_hbm, relt_hbm, wg_hbm, wu_hbm, wd_hbm,
-    idrow_out, grads_out, negg_out,
+    owner_hbm, local_hbm, rel_hbm, neg_hbm, gin_hbm, gout_hbm, tab_hbm, relt_hbm, wg_hbm, wu_hbm, wd_hbm,
+    idrow_out, back, negg_out,
+    owner_ref, local_ref, rel_ref, neg_ref, gin_ref, gout_ref,
     tab_f, tab_b, relt, wg, wu, wd,
-    ids_s, ids_r, col_s, rows_s, rows_r, outg, back,
+    ids_s, ids_r, col_s, idrow_s, rows_s, rows_r, outg,
     negs, qring, part_s, part_r, sums, base_s, gate_s, up_s, qvec_s, mix_s, acc_s, ctx_s,
     load_sem, a2a_send, a2a_recv, nsend, nrecv, rsend, rrecv,
 ):
     me_e, me_g = lax.axis_index("ent"), lax.axis_index("grp")
     me = me_e * GRP + me_g
 
-    barrier = pltpu.get_barrier_semaphore()
-
-    others = [lax.rem(me_g + k, GRP) for k in range(GRP)]
-
-    def each_peer(act, lo=0, hi=ENT):
-        def across(j, carry):
-            e = lax.rem(me_e + j, ENT)
-            for g in others[1:]:
-                act(e, g)
-            return carry
-
-        def along(j, carry):
-            act(lax.rem(me_e + j, ENT), me_g)
-            return carry
-
-        lax.fori_loop(lo, hi, across, 0)
-        lax.fori_loop(max(lo, 1), hi, along, 0)
-
-    each_peer(
-        lambda e, g: pl.semaphore_signal(barrier, inc=1, device_id=(e, g), device_id_type=MESH)
-    )
-
     loads = [
         pltpu.make_async_copy(src, dst, load_sem.at[i])
         for i, (src, dst) in enumerate(
-            ((tab_hbm, tab_f), (relt_hbm, relt), (wg_hbm, wg), (wu_hbm, wu), (wd_hbm, wd))
+            (
+                (owner_hbm, owner_ref), (local_hbm, local_ref), (neg_hbm, neg_ref), (rel_hbm, rel_ref),
+                (gin_hbm, gin_ref), (gout_hbm, gout_ref),
+                (tab_hbm, tab_f), (relt_hbm, relt), (wg_hbm, wg), (wu_hbm, wu), (wd_hbm, wd),
+            )
         )
     ]
     for load in loads:
         load.start()
+
+    barrier = pltpu.get_barrier_semaphore()
+
+    span = lambda k: min(k, SIDE - k)
+    away = sorted(range(1, GRP), key=lambda k: -(span(k // SIDE) + span(k % SIDE)))
+    others = [
+        lax.rem(me_g // SIDE + k // SIDE, SIDE) * SIDE + lax.rem(me_g % SIDE + k % SIDE, SIDE) for k in away
+    ]
+
+    def each_peer(act, lo=0, hi=ENT):
+        def across(j, carry):
+            e = lax.rem(me_e + (j + ENT // 2), ENT)
+            for g in others:
+                act(e, g)
+            return carry
+
+        def along(j, carry):
+            act(lax.rem(me_e + (j + ENT // 2), ENT), me_g)
+            return carry
+
+        lax.fori_loop(lo, hi, across, 0)
+        lax.fori_loop(lo, min(hi, ENT // 2), along, 0)
+        lax.fori_loop(max(lo, ENT // 2 + 1), hi, along, 0)
+
+    each_peer(
+        lambda e, g: pl.semaphore_signal(barrier, inc=1, device_id=(e, g), device_id_type=MESH)
+    )
 
     def exchange(n, src, dst, lo=0, hi=ENT):
         def send(e, g):
@@ -187,13 +197,13 @@
             ).start()
 
         each_peer(send, lo, hi)
-        if lo == 0:
-            dst[me] = src[me]
 
     def wait_all(buf, sem):
         view = buf.at[pl.ds(0, DEV - 1)]
         pltpu.make_async_copy(view, view, sem).wait()
 
+    for load in loads[:6]:
+        load.wait()
     owner = owner_ref[...]
     local = local_ref[...]
     owner_t = hot(iota((DEV, REFS), 0) == owner)
@@ -212,7 +222,7 @@
     )
     ids_s[...] = ids.reshape(DEV, 1, 128)
 
-    loads[0].wait()
+    loads[6].wait()
 
     def narrow(i, carry):
         part = pl.ds(pl.multiple_of(i * 256, 256), 256)
@@ -226,6 +236,7 @@
 
     pl.semaphore_wait(barrier, DEV - 1)
     exchange(0, ids_s, ids_r)
+    ids_r[me] = ids_s[me]
     ag_n.stage0()
 
     wait_all(ids_r, a2a_recv.at[0])
@@ -239,25 +250,31 @@
     ids_col = jnp.sum(256.0 * slot_high + slot_low, axis=1, keepdims=True)
     col_s[...] = jnp.broadcast_to(ids_col, (SLOTS, 128))
     ones = jnp.ones((8, 128), BF)
-    idrow_out[...] = 256.0 * nt(ones, slot_high.astype(BF)) + nt(ones, slot_low.astype(BF))
+    idrow_s[...] = 256.0 * nt(ones, slot_high.astype(BF)) + nt(ones, slot_low.astype(BF))
 
     ag_n.stage1()
 
+    keep_ids = pltpu.make_async_copy(idrow_s, idrow_out, load_sem.at[0])
+    keep_ids.start()
+
     def look(i, carry):
-        part = pl.ds(pl.multiple_of(i * 256, 256), 256)
+        part = pl.ds(pl.multiple_of(i * LOOK, LOOK), LOOK)
         want = col_s[part, :][:, :1].astype(I32)
-        found = nn(hot(want == iota((256, ROWS), 1)), tab_b[...])
-        rows_s[pl.ds(i * 32, 32)] = found.reshape(32, CAP, D).astype(BF)
+        found = nn(hot(want == iota((LOOK, ROWS), 1)), tab_b[...])
+        n = LOOK // CAP
+        rows_s[pl.ds(i * n, n)] = found.reshape(n, CAP, D).astype(BF)
         return carry
 
-    lax.fori_loop(0, SLOTS // 256, look, 0)
+    lax.fori_loop(0, SLOTS // LOOK, look, 0)
     exchange(1, rows_s, rows_r)
+    rows_r[me] = rows_s[me]
+    for h in (0, 1):
+        ag_n.second(h, 1)
     ag_n.across(0)
     ag_n.stage2()
     ag_n.across(-1)
-    ag_n.across(1)
-
-    loads[1].wait()
+
+    loads[7].wait()
     rel_col = column(rel_ref[...].astype(F32))[:, :1].astype(I32)
     rel_rows = nn(hot(rel_col == iota((Q, NREL), 1)), relt[...])
     slot_col = column(slot_row.astype(F32))[:, :1].astype(I32)
@@ -266,27 +283,31 @@
     wait_all(rows_r, a2a_recv.at[1])
     came = rows_r[...].astype(F32).reshape(SLOTS, D).astype(BF)
     fetched = nn(pick, came)
-    ag_n.across(2)
     ctx_s[...] = fetched[Q:]
     base = fetched[:Q] + rel_rows
     base_s[...] = base
     r1 = lax.rsqrt(jnp.mean(base * base, axis=-1, keepdims=True) + EPS)
     normed = (base * r1 * gin_ref[...]).astype(BF)
     acc_s[...] = jnp.zeros((Q, D), F32)
-    for load in loads[2:]:
+    for load in loads[8:]:
         load.wait()
 
-    def ahead(i, carry):
-        part = pl.ds(pl.multiple_of(i * FC, FC), FC)
+    def ahead(i):
+        part = slice(i * FC, i * FC + FC)
         g = nn(normed, wg[:, part])
         u = nn(normed, wu[:, part])
-        gate_s[:, part] = g
-        up_s[:, part] = u
-        hidden = (g * jax.nn.sigmoid(g) * u).astype(BF)
+        s = jax.nn.sigmoid(g)
+        silu = g * s
+        up_s[:, part] = silu
+        gate_s[:, part] = u * (s + silu * (1.0 - s))
+        hidden = (silu * u).astype(BF)
         acc_s[...] += nn(hidden, wd[part, :])
-        return carry
-
-    lax.fori_loop(0, NFC, ahead, 0)
+
+    for i in range(NFC // 2):
+        ahead(i)
+    ag_n.across(1)
+    for i in range(NFC // 2, NFC):
+        ahead(i)
     mixed = base_s[...] + acc_s[...]
     r2 = lax.rsqrt(jnp.mean(mixed * mixed, axis=-1, keepdims=True) + EPS)
     query_vec = mixed * r2 * gout_ref[...]
@@ -307,16 +328,20 @@
     def arrive(view, sem):
         pltpu.make_async_copy(view, view, rrecv.at[sem]).wait()
 
-    ahead_of = lambda i, k: lax.rem(i + k, SIDE)
-    rings = [
-        (z, ahead_of(z, 1), ahead_of(z, 3), x * SIDE + ahead_of(z, 1), x * SIDE + ahead_of(z, 3)),
-        (x, ahead_of(x, 1), ahead_of(x, 3), ahead_of(x, 1) * SIDE + z, ahead_of(x, 3) * SIDE + z),
-    ]
+    odd = lax.rem(me_e, 2)
+    even = 1 - odd
+    here, line = z * even + x * odd, x * even + z * odd
+
+    def along(k):
+        i = lax.rem(here + k, SIDE)
+        return i, (x * even + i * odd) * SIDE + (i * even + z * odd)
+
+    def across(k):
+        i = lax.rem(line + k, SIDE)
+        return (i * even + x * odd) * SIDE + (z * even + i * odd)
+
+    (nxt, after), (prev, ahead_me), (opposite, _) = along(1), along(3), along(2)
     first, second = pl.ds(0, 128), pl.ds(128, 128)
-    for k, (own, _, _, after, before_me) in enumerate(rings):
-        qring[k, own] = query_b
-        hop(qring.at[k, own], qring.at[k, own], 8 * k, after)
-        hop(qring.at[k, own], qring.at[k, own], 8 * k + 1, before_me)
 
     def against(own, blocks):
         total = None
@@ -330,13 +355,22 @@
     def neg_at(dx, dz):
         return negs[lax.rem(x + (dx + SIDE), SIDE) * SIDE + lax.rem(z + (dz + SIDE), SIDE)]
 
-    def near(i, carry):
-        acc_s[...] += against(query_b, [neg_at(i - 1, dz) for dz in (-1, 0, 1)])
-        return carry
-
-    acc_s[...] = jnp.zeros((Q, D), F32)
-    lax.fori_loop(0, 3, near, 0)
+    acc_s[...] = against(query_b, [neg_at(dx, dz) for dx in (-1, 0) for dz in (-1, 0, 1)])
+    ag_n.across(2)
+    qring[here] = query_b
+    hop(qring.at[here], qring.at[here], 0, after)
+    hop(qring.at[here], qring.at[here], 1, ahead_me)
+    acc_s[...] += against(query_b, [neg_at(1, dz) for dz in (-1, 0, 1)])
+
+    def lent(*ks):
+        return jnp.concatenate([negs[across(k)] for k in ks], axis=0)
+
+    sums[...] = against(lent(1, 3, 0), [query_b])
     ag_n.finish()
+    arrive(qring.at[prev], 0)
+    hop(qring.at[prev, first], qring.at[prev, first], 2, after)
+    arrive(qring.at[nxt], 1)
+    hop(qring.at[nxt, second], qring.at[nxt, second], 3, ahead_me)
     acc_s[...] += against(query_b, [neg_at(dx, 2) for dx in (-1, 0, 1)])
     acc_s[...] += against(query_b, [neg_at(2, dz) for dz in (-1, 0, 1, 2)])
 
@@ -353,24 +387,21 @@
     d_mixed_b = d_mixed.astype(BF)
     acc_s[...] = jnp.zeros((Q, D), F32)
 
-    def behind(i, carry):
-        part = pl.ds(pl.multiple_of(i * FC, FC), FC)
-        g = gate_s[:, part]
-        u = up_s[:, part]
-        s = jax.nn.sigmoid(g)
+    def behind(i):
+        part = slice(i * FC, i * FC + FC)
         dh = nt(d_mixed_b, wd[part, :]).astype(BF).astype(F32)
-        du = (dh * (g * s)).astype(BF)
-        dg = (dh * u * (s * (1.0 + g * (1.0 - s)))).astype(BF)
+        du = (dh * up_s[:, part]).astype(BF)
+        dg = (dh * gate_s[:, part]).astype(BF)
         acc_s[...] += nt(dg, wg[:, part]) + nt(du, wu[:, part])
-        return carry
-
-    lax.fori_loop(0, NFC // 2, behind, 0)
-    for k, (_, nxt, prev, after, before_me) in enumerate(rings):
-        arrive(qring.at[k, prev], 8 * k)
-        hop(qring.at[k, prev, first], qring.at[k, prev, first], 8 * k + 2, after)
-        arrive(qring.at[k, nxt], 8 * k + 1)
-        hop(qring.at[k, nxt, second], qring.at[k, nxt, second], 8 * k + 3, before_me)
-    lax.fori_loop(NFC // 2, NFC, behind, 0)
+
+    for i in range(NFC - 1):
+        behind(i)
+    arrive(qring.at[opposite, first], 2)
+    arrive(qring.at[opposite, second], 3)
+    part_s[0] = against(lent(2), [qring[i] for i in range(SIDE)]).astype(BF)
+    hop(part_s.at[0, first], part_r.at[0, first], 4, across(1))
+    hop(part_s.at[0, second], part_r.at[0, second], 5, across(3))
+    behind(NFC - 1)
     base = base_s[...]
     r1 = lax.rsqrt(jnp.mean(base * base, axis=-1, keepdims=True) + EPS)
     t1 = acc_s[...] * gin_ref[...]
@@ -381,40 +412,26 @@
     place = hot(iota((SLOTS, REFS), 0) == slot_row)
     out = nn(place[:, :Q], head_b) + nn(place[:, Q:], ctx_b)
     outg[...] = out.reshape(DEV, CAP, D).astype(BF)
-    exchange(2, outg, back, 0, ENT // 2)
-
-    upper, lower = pl.ds(0, 64), pl.ds(64, 64)
-    for h in (0, 1):
-        arrive(qring.at[h, 0, first], 8 * h + 2)
-        arrive(qring.at[h, 0, second], 8 * h + 3)
-        own = jnp.concatenate(
-            [negs[ag_n.block(h, a, 0), h * 128 : h * 128 + 128] for a in (2, 1, -1, 0)], axis=0
-        )
-        terms = against(own, [qring[h, i] for i in range(SIDE)])
-        part_s[h, 0] = terms[:128].astype(BF)
-        sums[h] = terms[128:]
-        _, _, _, after, before_me = rings[1 - h]
-        hop(part_s.at[h, 0, upper], part_r.at[h, 0, upper], 8 * h + 4, after)
-        hop(part_s.at[h, 0, lower], part_r.at[h, 0, lower], 8 * h + 5, before_me)
-    exchange(2, outg, back, ENT // 2, ENT)
-    for h in (0, 1):
-        _, _, _, after, before_me = rings[1 - h]
-        arrive(part_r.at[h, 0, upper], 8 * h + 4)
-        part_s[h, 1, :64] = (sums[h, :64] + part_r[h, 0, :64].astype(F32)).astype(BF)
-        part_s[h, 1, 64:] = sums[h, 64:128].astype(BF)
-        hop(part_s.at[h, 1], part_r.at[h, 1], 8 * h + 6, after)
-        arrive(part_r.at[h, 0, lower], 8 * h + 5)
-        part_s[h, 2, :64] = sums[h, 128:192].astype(BF)
-        part_s[h, 2, 64:] = (sums[h, 192:256] + part_r[h, 0, 64:].astype(F32)).astype(BF)
-        hop(part_s.at[h, 2], part_r.at[h, 2], 8 * h + 7, before_me)
-    for h in (0, 1):
-        arrive(part_r.at[h, 1], 8 * h + 6)
-        arrive(part_r.at[h, 2], 8 * h + 7)
-        total = sums[h, 256:] + (part_r[h, 1].astype(F32) + part_r[h, 2].astype(F32))
-        negg_out[h * 128 : h * 128 + 128, :] = total.astype(BF)
+    exchange(2, outg, back)
+    keep = pltpu.make_async_copy(outg.at[me], back.at[me], load_sem.at[1])
+    keep.start()
+
+    sums[...] += against(lent(1, 3, 0), [qring[prev], qring[nxt], qring[opposite]])
+    arrive(part_r.at[0, first], 4)
+    part_s[1, :128] = (sums[:128] + part_r[0, :128].astype(F32)).astype(BF)
+    part_s[1, 128:] = sums[128:256].astype(BF)
+    hop(part_s.at[1], part_r.at[1], 6, across(1))
+    arrive(part_r.at[0, second], 5)
+    part_s[2, :128] = sums[256:384].astype(BF)
+    part_s[2, 128:] = (sums[384:512] + part_r[0, 128:].astype(F32)).astype(BF)
+    hop(part_s.at[2], part_r.at[2], 7, across(3))
+    arrive(part_r.at[1], 6)
+    arrive(part_r.at[2], 7)
+    negg_out[...] = (sums[512:] + (part_r[1].astype(F32) + part_r[2].astype(F32))).astype(BF)
 
     wait_all(back, a2a_recv.at[2])
-    grads_out[...] = back[...].astype(F32).reshape(SLOTS, D).astype(BF)
+    keep.wait()
+    keep_ids.wait()
     wait_all(ids_s, a2a_send.at[0])
     wait_all(rows_s, a2a_send.at[1])
     wait_all(outg, a2a_send.at[2])
@@ -423,11 +440,15 @@
         copy.wait_send()
 
 
-def place_kernel(idrow_ref, grads_ref, neg_ref, negg_ref, out_ref):
+def place_kernel(idrow_ref, back_ref, neg_ref, negg_ref, out_ref, grads):
+    @pl.when(pl.program_id(0) == 0)
+    def _():
+        grads[...] = back_ref[...].astype(F32).reshape(SLOTS, D).astype(BF)
+
     start = pl.program_id(0) * TILE
     slots = hot(iota((TILE, SLOTS), 0) + start == idrow_ref[...][:1, :].astype(I32))
     spans = hot(iota((TILE, Q), 0) + start == neg_ref[...])
-    out_ref[...] = nn(slots, grads_ref[...]) + nn(spans, negg_ref[...])
+    out_ref[...] = nn(slots, grads[...]) + nn(spans, negg_ref[...])
 
 
 def per_device(table, touch_owner, touch_local, query_rel, neg_local, rel_table, in_gain, out_gain, w_gate, w_up, w_down):
@@ -438,12 +459,18 @@
         step_kernel,
         out_shape=(
             jax.ShapeDtypeStruct((8, SLOTS), F32),
-            jax.ShapeDtypeStruct((SLOTS, D), BF),
+            jax.ShapeDtypeStruct((DEV, CAP, D), BF),
             jax.ShapeDtypeStruct((Q, D), BF),
         ),
-        in_specs=[vmem] * 6 + [hbm] * 5,
-        out_specs=(vmem, vmem, vmem),
+        in_specs=[hbm] * 11,
+        out_specs=(hbm, hbm, vmem),
         scratch_shapes=[
+            pltpu.VMEM((1, REFS), I32),
+            pltpu.VMEM((1, REFS), I32),
+            pltpu.VMEM((1, Q), I32),
+            pltpu.VMEM((1, Q), I32),
+            pltpu.VMEM((1, D), F32),
+            pltpu.VMEM((1, D), F32),
             pltpu.VMEM((ROWS, D), F32),
             pltpu.VMEM((ROWS, D), BF),
             pltpu.VMEM((NREL, D), BF),
@@ -453,15 +480,15 @@
             pltpu.VMEM((DEV, 1, 128), F32),
             pltpu.VMEM((DEV, 1, 128), F32),
             pltpu.VMEM((SLOTS, 128), F32),
-            pltpu.VMEM((DEV, CAP, D), BF),
+            pltpu.VMEM((8, SLOTS), F32),
             pltpu.VMEM((DEV, CAP, D), BF),
             pltpu.VMEM((DEV, CAP, D), BF),
             pltpu.VMEM((DEV, CAP, D), BF),
             pltpu.VMEM((GRP, Q, D), BF),
-            pltpu.VMEM((2, SIDE, Q, D), BF),
-            pltpu.VMEM((2, 3, 128, D), BF),
-            pltpu.VMEM((2, 3, 128, D), BF),
-            pltpu.VMEM((2, 384, D), F32),
+            pltpu.VMEM((SIDE, Q, D), BF),
+            pltpu.VMEM((3, Q, D), BF),
+            pltpu.VMEM((3, Q, D), BF),
+            pltpu.VMEM((768, D), F32),
             pltpu.VMEM((Q, D), F32),
             pltpu.VMEM((Q, FF), F32),
             pltpu.VMEM((Q, FF), F32),
@@ -469,13 +496,13 @@
             pltpu.VMEM((Q, D), F32),
             pltpu.VMEM((Q, D), F32),
             pltpu.VMEM((Q, D), F32),
-            pltpu.SemaphoreType.DMA((5,)),
+            pltpu.SemaphoreType.DMA((11,)),
             pltpu.SemaphoreType.DMA((3,)),
             pltpu.SemaphoreType.DMA((3,)),
             pltpu.SemaphoreType.DMA((40,)),
             pltpu.SemaphoreType.DMA((64,)),
-            pltpu.SemaphoreType.DMA((16,)),
-            pltpu.SemaphoreType.DMA((16,)),
+            pltpu.SemaphoreType.DMA((8,)),
+            pltpu.SemaphoreType.DMA((8,)),
         ],
         compiler_params=pltpu.CompilerParams(
             collective_id=0, has_side_effects=True, vmem_limit_bytes=60 * 1024 * 1024
@@ -499,8 +526,9 @@
         place_kernel,
         grid=(ROWS // TILE,),
         out_shape=jax.ShapeDtypeStruct((ROWS, D), F32),
-        in_specs=[whole((8, SLOTS)), whole((SLOTS, D)), whole((1, Q)), whole((Q, D))],
+        in_specs=[whole((8, SLOTS)), pl.BlockSpec((DEV, CAP, D), lambda i: (0, 0, 0)), whole((1, Q)), whole((Q, D))],
         out_specs=pl.BlockSpec((TILE, D), lambda i: (i, 0)),
+        scratch_shapes=[pltpu.VMEM((SLOTS, D), BF)],
         name="place",
     )(idrow, grads, neg_row, negg)
 

time: 83.1 us -> 81.1 us (0.976)
  Pallas kernels: 83 us -> 80.9 us
    pallas_call x1, Pallas kernels: 77.2 us -> 75 us  [per_device(): pl.pallas_call(step_kernel, out_shape=(jax.ShapeDtypeStruct((8, SLOTS), F...]
where the time goes in v3:
time: 81.1 us; the launch traced here: 80.9 us
  Pallas kernels  80.9 us (100%)
    pallas_call x1, Pallas kernels, per_device(): pl.pallas_call(step_kernel, out_shape=(jax.ShapeDtypeStruct((8, SLOTS), F...  75 us
    pallas_call x1, Pallas kernels, per_device(): pl.pallas_call(place_kernel, grid=(ROWS // TILE,), out_shape=jax.ShapeDty...  5.88 us

profile of v3, /device:TPU:1, one launch (start us, length us, event | category | flops | bytes accessed | tf_op | source)
XLA Modules:
  0.0 80.9 jit_solution(12125479803069495455)
XLA Ops:
  0.0 75.0 %step.1 = (f32[8,1024]{1,0:T(8,128)}, bf16[128,8,512]{2,1,0:T(8,128)(2,1)}, bf16[256,512]{1,0:T(8,128)(2,1)}) custom-call(s32[1,512]{1,0:T(1,128)} %bitcast.8, s32[1,512]{1,0:T(1,128)} %bitcast.9, s32[1,256]{1,0:T(1,128)} %bitcast.12, s32[1,256]{1,0:T(1,128)} %bitcast.6, f32[1,512]{1,0:T(1,128)} %bitcast.10, f32[1,512]{1,0:T(1,128)} %bitcast.11, ...), custom_call_target="tpu_custom_call" | custom-call | tf_op jit(solution)/shard_map/step/pallas_call | solution.py:458
  75.1 5.9 %place.1 = f32[2048,512]{1,0:T(8,128)} custom-call(f32[8,1024]{1,0:T(8,128)} %get-tuple-element.8.idrow_ref, bf16[128,8,512]{2,1,0:T(8,128)(2,1)} %get-tuple-element.9.back_ref, s32[1,256]{1,0:T(1,128)} %bitcast.7, bf16[256,512]{1,0:T(8,128)(2,1)} %get-tuple-element.10.negg_ref), custom_call_target="tpu_custom_call" | custom-call | tf_op jit(solution)/shard_map/place/pallas_call | solution.py:525

commit v4 on v3

--- a/solution.py
+++ b/solution.py
@@ -28,7 +28,7 @@
 NFC = FF // FC
 ROWS = 2048
 NREL = 822
-TILE = 512
+TILE = 1024
 LOOK = 512
 INV = 1.0 / math.sqrt(D)
 
@@ -367,12 +367,13 @@
 
     sums[...] = against(lent(1, 3, 0), [query_b])
     ag_n.finish()
+    acc_s[...] += against(query_b, [neg_at(dx, 2) for dx in (-1, 0, 1)])
+    acc_s[...] += against(query_b, [neg_at(2, dz) for dz in (-1, 0, 1, 2)])
+
     arrive(qring.at[prev], 0)
     hop(qring.at[prev, first], qring.at[prev, first], 2, after)
     arrive(qring.at[nxt], 1)
     hop(qring.at[nxt, second], qring.at[nxt, second], 3, ahead_me)
-    acc_s[...] += against(query_b, [neg_at(dx, 2) for dx in (-1, 0, 1)])
-    acc_s[...] += against(query_b, [neg_at(2, dz) for dz in (-1, 0, 1, 2)])
 
     query_vec = qvec_s[...]
     ctx = ctx_s[...]
@@ -394,14 +395,13 @@
         dg = (dh * gate_s[:, part]).astype(BF)
         acc_s[...] += nt(dg, wg[:, part]) + nt(du, wu[:, part])
 
-    for i in range(NFC - 1):
+    for i in range(NFC):
         behind(i)
     arrive(qring.at[opposite, first], 2)
     arrive(qring.at[opposite, second], 3)
     part_s[0] = against(lent(2), [qring[i] for i in range(SIDE)]).astype(BF)
     hop(part_s.at[0, first], part_r.at[0, first], 4, across(1))
     hop(part_s.at[0, second], part_r.at[0, second], 5, across(3))
-    behind(NFC - 1)
     base = base_s[...]
     r1 = lax.rsqrt(jnp.mean(base * base, axis=-1, keepdims=True) + EPS)
     t1 = acc_s[...] * gin_ref[...]

time: 81.1 us -> 80.4 us (level)
  Pallas kernels: 80.9 us -> 79.9 us
    pallas_call x1, Pallas kernels: 75 us -> 74.2 us  [per_device(): pl.pallas_call(step_kernel, out_shape=(jax.ShapeDtypeStruct((8, SLOTS), F...]
where the time goes in v4:
time: 80.4 us; the launch traced here: 80 us
  Pallas kernels  79.9 us (99%)
    pallas_call x1, Pallas kernels, per_device(): pl.pallas_call(step_kernel, out_shape=(jax.ShapeDtypeStruct((8, SLOTS), F...  74.2 us
    pallas_call x1, Pallas kernels, per_device(): pl.pallas_call(place_kernel, grid=(ROWS // TILE,), out_shape=jax.ShapeDty...  5.77 us

profile of v4, /device:TPU:1, one launch (start us, length us, event | category | flops | bytes accessed | tf_op | source)
XLA Modules:
  0.0 80.0 jit_solution(9469896177934081053)
XLA Ops:
  0.0 74.2 %step.1 = (f32[8,1024]{1,0:T(8,128)}, bf16[128,8,512]{2,1,0:T(8,128)(2,1)}, bf16[256,512]{1,0:T(8,128)(2,1)}) custom-call(s32[1,512]{1,0:T(1,128)} %bitcast.8, s32[1,512]{1,0:T(1,128)} %bitcast.9, s32[1,256]{1,0:T(1,128)} %bitcast.12, s32[1,256]{1,0:T(1,128)} %bitcast.6, f32[1,512]{1,0:T(1,128)} %bitcast.10, f32[1,512]{1,0:T(1,128)} %bitcast.11, ...), custom_call_target="tpu_custom_call" | custom-call | tf_op jit(solution)/shard_map/step/pallas_call | solution.py:458
  74.2 5.8 %place.1 = f32[2048,512]{1,0:T(8,128)} custom-call(f32[8,1024]{1,0:T(8,128)} %get-tuple-element.8.idrow_ref, bf16[128,8,512]{2,1,0:T(8,128)(2,1)} %get-tuple-element.9.back_ref, s32[1,256]{1,0:T(1,128)} %bitcast.7, bf16[256,512]{1,0:T(8,128)(2,1)} %get-tuple-element.10.negg_ref), custom_call_target="tpu_custom_call" | custom-call | tf_op jit(solution)/shard_map/place/pallas_call | solution.py:525
